TPU v7x, 512 devices: a whole 4x4x16 slice. The times are simulated.
512 devices in a mesh: seq: 32 (over x, y, core), heads: 4 (over z_lo), dp: 4 (over z_hi).
Axes of the slice: x: 4, y: 4, z: 16 (z_hi: 4, z_lo: 4; z = z_hi * 4 + z_lo), core: 2. Of those that a mesh axis runs over, the one named last changes fastest.
Arguments:
- activations: bfloat16 [16384, 8192], P(('dp', 'seq'), 'heads'), parts along dimension 0, may hold values from -6 to 6
- conv_taps: bfloat16 [4, 8192], P(None, 'heads'), may hold values from -3 to 3
- gate_in: bfloat16 [8192, 1024], P('heads', 'seq'), may hold values from -0.0625 to 0.0625
- gate_out: bfloat16 [1024, 8], replicated, may hold values from -0.59765625 to 0.59765625
- queries: bfloat16 [16384, 8192], P(('dp', 'seq'), 'heads'), parts along dimension 0, may hold values from -1000 to 1000, as said below
- key_vectors: bfloat16 [16384, 1024], P(('dp', 'seq'), 'heads'), parts along dimension 0, may hold values from -4 to 4, as said below
- value_vectors: bfloat16 [16384, 1024], P(('dp', 'seq'), 'heads'), parts along dimension 0, may hold values from -6 to 6
- segment_ids: int32 [16384], P('dp'), parts along dimension 0, may hold values from 0 to 3, never falling along the last dimension, each value on 1 to 2048 neighbouring positions
Outputs:
- attended: bfloat16 [16384, 8192], P(('dp', 'seq'), 'heads'), parts along dimension 0
- key_mass: bfloat16 [8, 16384], P('heads', ('dp', 'seq')), parts along dimension 1
There are 4 independent parts, one for each index of `dp`. A program takes and returns all parts, laid end to end along the dimension named above; an argument that names none is the same for every part. Nothing has to cross between parts.
Inputs may be any that keep to these rules, and one draw needn't show every extreme that they name: `queries`: finite. `key_vectors`: finite.
All inputs are finite; a program needn't handle non-finite values.
Results may differ from a plain program's by a relative error of at most 0.0056.
Values may be sent and summed in bfloat16 or wider, within the bound.
A program may use at most 64 MiB of HBM per device.

v0:
```python
import math
import jax
import jax.numpy as jnp
from jax import lax
from jax.sharding import PartitionSpec as P

QUERY_HEADS = 64
KV_HEADS = 8
HEAD_DIM = 128
NEG_FILL = -1e30


def from_behind(block, axis, distance):
    devices = range(lax.axis_size(axis))
    route = [(i - distance, i) for i in devices if i - distance in devices]
    return lax.ppermute(block, axis, route)


def partner(x, axis, distance):
    return lax.ppermute(x, axis, [(i, i ^ 1 << distance) for i in range(lax.axis_size(axis))])


def key_places(flat_index, shard_rows, seq_count):
    half_rows = shard_rows // 2
    owner_dev = flat_index // shard_rows
    within = flat_index % shard_rows
    block_index = jnp.where(within < half_rows, 2 * owner_dev, 2 * seq_count - 1 - 2 * owner_dev)
    return block_index * half_rows + within % half_rows


def block_scores(query_heads, key_block, bias_block, allowed, score_scale):
    scores = (
        jnp.einsum("tgeh,kgh->getk", query_heads, key_block, preferred_element_type=jnp.float32)
        * score_scale
    )
    scores = scores + jnp.transpose(bias_block.astype(jnp.float32))[:, None, None, :]
    return jnp.where(allowed[None, None], scores, NEG_FILL)


def per_device(
    activations, conv_taps, gate_in, gate_out, queries, key_vectors, value_vectors, segment_ids
):
    shard_rows = activations.shape[0]
    tap_count = conv_taps.shape[0]
    rim_rows = from_behind(activations[shard_rows - (tap_count - 1) :], "seq", 1)
    widened = jnp.concatenate([rim_rows, activations], 0).astype(jnp.float32)
    summed = jnp.zeros(activations.shape, jnp.float32)
    for shift_back in range(tap_count):
        start_row = tap_count - 1 - shift_back
        summed = (
            summed
            + conv_taps[shift_back].astype(jnp.float32)
            * widened[start_row : start_row + shard_rows]
        )
    mixed_rows = summed.astype(jnp.bfloat16)
    partial_hidden = jnp.dot(
        mixed_rows,
        lax.all_gather(gate_in, "seq", axis=1, tiled=True),
        preferred_element_type=jnp.float32,
    )
    kv_local = key_vectors.shape[1] // HEAD_DIM
    group_size = QUERY_HEADS // KV_HEADS
    head_rank = lax.axis_index("heads")
    hidden = jax.nn.silu(lax.psum(partial_hidden, "heads")).astype(jnp.bfloat16)
    logits = jnp.dot(hidden, gate_out, preferred_element_type=jnp.float32)
    retention = lax.dynamic_slice_in_dim(
        jax.nn.log_sigmoid(logits).astype(jnp.bfloat16), head_rank * kv_local, kv_local, 1
    )
    seq_count = lax.axis_size("seq")
    seq_rank = lax.axis_index("seq")
    half_rows = shard_rows // 2
    local_index = jnp.arange(shard_rows, dtype=jnp.int32)
    moved_half = (
        queries[half_rows:],
        key_vectors[half_rows:],
        value_vectors[half_rows:],
        retention[half_rows:],
    )
    for bit_number in range(seq_count.bit_length() - 1):
        moved_half = partner(
            (moved_half[0], moved_half[1], moved_half[2], moved_half[3]), "seq", bit_number
        )
    own_queries = jnp.concatenate([queries[:half_rows], moved_half[0]], 0)
    own_keys = jnp.concatenate([key_vectors[:half_rows], moved_half[1]], 0)
    own_values = jnp.concatenate([value_vectors[:half_rows], moved_half[2]], 0)
    own_bias = jnp.concatenate([retention[:half_rows], moved_half[3]], 0)
    query_places = jnp.where(
        local_index < half_rows,
        2 * seq_rank * half_rows + local_index,
        (2 * seq_count - 1 - 2 * seq_rank) * half_rows + local_index - half_rows,
    )
    query_segments = jnp.take(segment_ids, query_places)
    query_heads = own_queries.reshape(shard_rows, kv_local, group_size, HEAD_DIM)
    score_scale = 1.0 / math.sqrt(HEAD_DIM)

    def visibility(flat_index):
        places = key_places(flat_index, shard_rows, seq_count)
        key_segments = jnp.take(segment_ids, places)
        return (places[None, :] <= query_places[:, None]) & (
            key_segments[None, :] == query_segments[:, None]
        )

    initial = (
        jnp.full((kv_local, group_size, shard_rows), NEG_FILL, jnp.float32),
        jnp.zeros((kv_local, group_size, shard_rows), jnp.float32),
    )
    all_keys, all_values, all_bias = (
        lax.all_gather(own_keys, "seq", axis=0, tiled=True),
        lax.all_gather(own_values, "seq", axis=0, tiled=True),
        lax.all_gather(own_bias, "seq", axis=0, tiled=True),
    )
    piece_rows = all_keys.shape[0]
    stats_block_width = math.gcd(piece_rows, 512)

    def one_block(block_number, state_in):
        offset = block_number * stats_block_width
        key_block = lax.dynamic_slice_in_dim(all_keys, offset, stats_block_width, 0).reshape(
            stats_block_width, kv_local, HEAD_DIM
        )
        bias_block = lax.dynamic_slice_in_dim(all_bias, offset, stats_block_width, 0)
        allowed = visibility(0 + offset + jnp.arange(stats_block_width, dtype=jnp.int32))

        def update(state_old):
            peak_old, mass_old = state_old
            masked = block_scores(query_heads, key_block, bias_block, allowed, score_scale)
            peak_new = jnp.maximum(peak_old, jnp.max(masked, axis=3))
            exponent = jnp.where(allowed[None, None], jnp.exp(masked - peak_new[..., None]), 0.0)
            return (peak_new, mass_old * jnp.exp(peak_old - peak_new) + jnp.sum(exponent, axis=3))

        def keep_state(state_old):
            return state_old

        return lax.cond(jnp.any(allowed), update, keep_state, state_in)

    row_peak, total_mass = lax.fori_loop(0, piece_rows // stats_block_width, one_block, initial)
    total_keys = all_keys.shape[0]
    block_width = math.gcd(total_keys, 512)
    block_count = total_keys // block_width
    key_blocks = all_keys.reshape(block_count, block_width, kv_local, HEAD_DIM)
    value_blocks = all_values.reshape(block_count, block_width, kv_local, HEAD_DIM)
    bias_blocks = all_bias.reshape(block_count, block_width, kv_local)

    def second_pass(accumulated, block_items):
        block_number, key_block, value_block, bias_block = block_items
        allowed = visibility(block_number * block_width + jnp.arange(block_width, dtype=jnp.int32))

        def attend(accum_in):
            masked = block_scores(query_heads, key_block, bias_block, allowed, score_scale)
            weights = (
                jnp.where(allowed[None, None], jnp.exp(masked - row_peak[..., None]), 0.0)
                / total_mass[..., None]
            )
            accum_out = accum_in + jnp.einsum(
                "getk,kgh->tgeh",
                weights.astype(jnp.bfloat16),
                value_block,
                preferred_element_type=jnp.float32,
            )
            return (accum_out, jnp.transpose(jnp.sum(weights, axis=(1, 2))) / group_size)

        def skip_block(accum_in):
            return (accum_in, jnp.zeros((block_width, kv_local), jnp.float32))

        return lax.cond(jnp.any(allowed), attend, skip_block, accumulated)

    accumulated, mass_blocks = lax.scan(
        second_pass,
        jnp.zeros((shard_rows, kv_local, group_size, HEAD_DIM), jnp.float32),
        (jnp.arange(block_count, dtype=jnp.int32), key_blocks, value_blocks, bias_blocks),
    )
    key_term = mass_blocks.reshape(total_keys, kv_local)
    key_mass = lax.psum_scatter(key_term, "seq", scatter_dimension=0, tiled=True).astype(
        jnp.bfloat16
    )
    attended = accumulated.reshape(shard_rows, kv_local * group_size * HEAD_DIM).astype(
        jnp.bfloat16
    )
    returned = (attended[half_rows:], key_mass[half_rows:])
    for bit_number in range(seq_count.bit_length() - 1):
        returned = partner((returned[0], returned[1]), "seq", bit_number)
    attended = jnp.concatenate([attended[:half_rows], returned[0]], 0)
    key_mass = jnp.concatenate([key_mass[:half_rows], returned[1]], 0)
    return (attended, jnp.transpose(key_mass))


def solution(mesh):
    return jax.shard_map(
        per_device,
        mesh=mesh,
        in_specs=(
            P(("dp", "seq"), "heads"),
            P(None, "heads"),
            P("heads", "seq"),
            P(),
            P(("dp", "seq"), "heads"),
            P(("dp", "seq"), "heads"),
            P(("dp", "seq"), "heads"),
            P("dp"),
        ),
        out_specs=(P(("dp", "seq"), "heads"), P("heads", ("dp", "seq"))),
        check_vma=False,
    )
```

profile of v0, /device:TPU:32, one launch (start us, length us, event | category | flops | bytes accessed | tf_op | source)
XLA Modules:
  0.0 626.7 jit_solution(121066509790797617)
XLA Ops:
  12.6 64.0 %all-gather.6.cloned.1.call-done = bf16[2048,1024]{0,1:T(8,128)(2,1)} async-done(((bf16[2048,32]{0,1:T(8,128)(2,1)}), bf16[2048,1024]{0,1:T(8,128)(2,1)}) %all-gather.6.cloned.1.call-update) | async-done | bytes 4194320 | tf_op jit(solution)/shard_map/all_gather | solution.py:58
  76.6 4.7 fusion.39
  84.6 3.1 collective-permute-start.1
  90.8 4.0 collective-permute-start.2
  94.8 3.7 collective-permute-done.2
  104.6 4.1 collective-permute-start.4
  108.8 3.5 collective-permute-done.4
  116.2 3.1 collective-permute-start.17
  122.0 4.0 collective-permute-start.18
  126.0 3.3 collective-permute-done.18
  129.3 3.1 collective-permute-start.19
  135.1 4.1 collective-permute-start.20
  139.1 3.2 collective-permute-done.20
  147.2 3.1 collective-permute-start.6
  150.3 12.8 %collective-permute-done.6 = bf16[64,2048]{0,1:T(8,128)(2,1)S(1)} collective-permute-done((bf16[64,2048]{0,1:T(8,128)(2,1)S(1)}, bf16[64,2048]{0,1:T(8,128)(2,1)S(1)}, u32[]{:S(2)}, u32[]{:S(2)}) %collective-permute-start.6) | collective-permute-done | bytes 262176 | tf_op jit(solution)/shard_map/ppermute | solution.py:20
  163.1 4.0 collective-permute-start.7
  167.1 13.2 %collective-permute-done.7 = bf16[64,2048]{0,1:T(8,128)(2,1)S(1)} collective-permute-done((bf16[64,2048]{0,1:T(8,128)(2,1)S(1)}, bf16[64,2048]{0,1:T(8,128)(2,1)S(1)}, u32[]{:S(2)}, u32[]{:S(2)}) %collective-permute-start.7) | collective-permute-done | bytes 262176 | tf_op jit(solution)/shard_map/ppermute | solution.py:20
  180.3 3.1 collective-permute-start.8
  183.4 11.0 %collective-permute-done.8 = bf16[64,2048]{0,1:T(8,128)(2,1)S(1)} collective-permute-done((bf16[64,2048]{0,1:T(8,128)(2,1)S(1)}, bf16[64,2048]{0,1:T(8,128)(2,1)S(1)}, u32[]{:S(2)}, u32[]{:S(2)}) %collective-permute-start.8) | collective-permute-done | bytes 262176 | tf_op jit(solution)/shard_map/ppermute | solution.py:20
  194.4 4.4 collective-permute-start.9
  208.8 3.5 collective-permute-start.13
  221.4 3.8 collective-permute-start.15
  228.3 49.2 %all-gather.8.cloned.1.call-done = bf16[4096,256]{1,0:T(8,128)(2,1)} async-done(((bf16[128,256]{1,0:T(8,128)(2,1)}), bf16[4096,256]{1,0:T(8,128)(2,1)}) %all-gather.8.cloned.1.call-update) | async-done | bytes 2097168 | tf_op jit(solution)/shard_map/all_gather | solution.py:109
  281.8 20.7 %all_gather.14 = bf16[4096,2]{0,1:T(2,128)(2,1)S(1)} all-gather(bf16[128,2]{0,1:T(2,128)(2,1)S(1)} %pad_maximum_fusion.4), channel_id=1, replica_groups=mesh['seq'=32,'heads'=4,'dp'=4] {'seq'}, dimensions={0}, use_global_device_ids=true | all-gather | bytes 16896 | tf_op jit(solution)/shard_map/all_gather | solution.py:110
  302.5 59.6 %while.38 = (s32[]{:T(128)}, f32[2,8,128]{2,1,0:T(8,128)S(1)}, f32[2,8,128]{2,1,0:T(8,128)S(1)}, s32[4096]{0:T(1024)S(1)}, s32[128]{0:T(128)S(1)}, /*index=5*/bf...) while((s32[]{:T(128)}, f32[2,8,128]{2,1,0:T(8,128)S(1)}, ...), condition=%wide.region_7.9_spmd.clone, body=%wide.region_1.8_spmd.clone.sunk | while | flops 279233152 | bytes 10043169 | solution.py:135
  302.5 3.1 gather_fusion
  307.3 3.4 conditional.6
  310.8 3.1 gather_fusion
  315.6 3.4 conditional.6
  319.1 3.1 gather_fusion
  323.9 3.4 conditional.6
  327.4 3.1 gather_fusion
  332.3 3.1 gather_fusion
  337.2 3.1 gather_fusion
  342.0 3.4 conditional.6
  345.5 3.1 gather_fusion
  350.3 3.4 conditional.6
  353.8 3.1 gather_fusion
  358.6 3.4 conditional.6
  362.2 75.0 %while.39 = (s32[]{:T(128)}, f32[128,2,8,128]{3,0,2,1:T(8,128)S(1)}, f32[8,512,2]{1,2,0:T(2,128)S(1)}, s32[8]{0:T(128)S(1)}, s32[4096]{0:T(1024)S(1)}, /*index=5...) while((s32[]{:T(128)}, ...), condition=%wide.region_13.15_spmd.clone, body=%wide.region_8.14_spmd.clone.sunk | while | flops 545829504 | bytes 7545635 | solution.py:166
  363.4 3.1 gather_fusion.1
  368.0 4.6 conditional.7
  374.0 3.1 gather_fusion.1
  378.6 4.6 conditional.7
  384.5 3.1 gather_fusion.1
  389.1 4.6 conditional.7
  395.0 3.1 gather_fusion.1
  401.0 3.1 gather_fusion.1
  406.9 3.1 gather_fusion.1
  411.5 4.6 conditional.7
  417.4 3.1 gather_fusion.1
  422.0 4.6 conditional.7
  428.0 3.1 gather_fusion.1
  432.6 4.6 conditional.7
  443.8 7.6 %collective-permute-done.22 = bf16[64,2048]{1,0:T(8,128)(2,1)S(1)} collective-permute-done((bf16[64,2048]{1,0:T(8,128)(2,1)S(1)}, bf16[64,2048]{1,0:T(8,128)(2,1)S(1)}, u32[]{:S(2)}, u32[]{:S(2)}) %collective-permute-start.22) | collective-permute-done | bytes 262176 | tf_op jit(solution)/shard_map/ppermute | solution.py:20
  451.5 4.3 collective-permute-start.23
  455.7 6.8 %collective-permute-done.23 = bf16[64,2048]{1,0:T(8,128)(2,1)S(1)} collective-permute-done((bf16[64,2048]{1,0:T(8,128)(2,1)S(1)}, bf16[64,2048]{1,0:T(8,128)(2,1)S(1)}, u32[]{:S(2)}, u32[]{:S(2)}) %collective-permute-start.23) | collective-permute-done | bytes 262176 | tf_op jit(solution)/shard_map/ppermute | solution.py:20
  462.5 18.0 %collective-permute-start.24 = (bf16[64,2048]{1,0:T(8,128)(2,1)S(1)}, bf16[64,2048]{1,0:T(8,128)(2,1)S(1)}, u32[]{:S(2)}, u32[]{:S(2)}) collective-permute-start(bf16[64,2048]{1,0:T(8,128)(2,1)S(1)} %collective-permute-done.23), channel_id=1, source_target_pairs={{0,128},{16,144},{32,160},{48,176},{64,192},{80,208},{96,224},{112... | collective-permute-start | bytes 786440 | tf_op jit(solution)/shard_map/ppermute | solution.py:20
  482.6 102.7 %reduce-scatter.4.cloned.1.call-done = f32[128,2]{1,0:T(8,128)} async-done(((f32[4096,2]{1,0:T(8,128)}), f32[128,2]{1,0:T(8,128)}) %reduce-scatter.4.cloned.1.call-update) | async-done | bytes 1040
  586.2 4.6 collective-permute-start.25
  595.8 3.5 collective-permute-done.27
  599.4 3.4 collective-permute-start.28
  602.7 3.6 collective-permute-done.28
  614.8 3.9 collective-permute-done.30
  (265 shorter events, 149.7 us)
Async XLA Ops:
  7.2 191.7 %copy-start = (bf16[1024,8]{0,1:T(8,128)(2,1)S(1)}, bf16[1024,8]{0,1:T(8,128)(2,1)}, u32[]{:S(2)}) copy-start(bf16[1024,8]{0,1:T(8,128)(2,1)} %param.21) | copy-start | bytes 49156
  7.2 69.4 %all-gather.6.cloned.1.call-start = ((), (), s32[]{:S(2)}) async-start(), calls=%async_computation.2 | async-start | bytes 4325376 | tf_op jit(solution)/shard_map/all_gather | solution.py:58
  7.9 190.9 %all-reduce.2.cloned.1.call-start = ((), (), s32[]{:S(2)}) async-start(), calls=%async_computation.3 | async-start | bytes 1048576 | tf_op jit(solution)/shard_map/psum | solution.py:64
  8.7 2.6 collective-permute-start.10
  76.6 4.8 copy-start.3
  76.6 36.5 %copy-start.4 = (bf16[128,256]{1,0:T(8,128)(2,1)S(1)}, bf16[128,256]{1,0:T(8,128)(2,1)}, u32[]{:S(2)}) copy-start(bf16[128,256]{1,0:T(8,128)(2,1)} %param.24) | copy-start | bytes 196612
  76.6 66.5 %copy-start.2 = (bf16[128,2048]{1,0:T(8,128)(2,1)S(1)}, bf16[128,2048]{1,0:T(8,128)(2,1)}, u32[]{:S(2)}) copy-start(bf16[128,2048]{1,0:T(8,128)(2,1)} %param.22) | copy-start | bytes 1572868
  81.3 120.9 %copy-start.1 = (s32[4096]{0:T(1024)S(1)}, s32[4096]{0:T(1024)}, u32[]{:S(2)}) copy-start(s32[4096]{0:T(1024)} %param.25) | copy-start | bytes 49156
  81.3 137.6 %all-gather.4.cloned.1.call-start = ((), (), s32[]{:S(2)}) async-start(), calls=%async_computation.1 | async-start | bytes 2162688 | tf_op jit(solution)/shard_map/all_gather | solution.py:108
  81.5 3.1 collective-permute-start
  84.6 6.1 collective-permute-start.1
  90.8 7.7 %collective-permute-start.2 = (bf16[64,256]{0,1:T(8,128)(2,1)S(1)}, bf16[64,256]{0,1:T(8,128)(2,1)S(1)}, u32[]{:S(2)}, u32[]{:S(2)}) collective-permute-start(bf16[64,256]{0,1:T(8,128)(2,1)S(1)} %collective-permute-done.1), channel_id=1, source_target_pairs={{0,64},{16,80},{32,96},{48,112},{64,0},{80,16},{96,32},{112,48},{1... | collective-permute-start | bytes 98312 | tf_op jit(solution)/shard_map/ppermute | solution.py:20
  98.4 6.1 collective-permute-start.3
  104.6 7.7 %collective-permute-start.4 = (bf16[64,256]{0,1:T(8,128)(2,1)S(1)}, bf16[64,256]{0,1:T(8,128)(2,1)S(1)}, u32[]{:S(2)}, u32[]{:S(2)}) collective-permute-start(bf16[64,256]{0,1:T(8,128)(2,1)S(1)} %collective-permute-done.3), channel_id=1, source_target_pairs={{0,256},{16,272},{32,288},{48,304},{64,320},{80,336},{96,352},{112... | collective-permute-start | bytes 98312 | tf_op jit(solution)/shard_map/ppermute | solution.py:20
  113.0 164.4 %all-gather.8.cloned.1.call-start = ((), (), s32[]{:S(2)}) async-start(), calls=%async_computation.4 | async-start | bytes 2162688 | tf_op jit(solution)/shard_map/all_gather | solution.py:109
  113.1 3.1 collective-permute-start.16
  116.2 5.8 collective-permute-start.17
  122.0 7.3 %collective-permute-start.18 = (bf16[64,256]{1,0:T(8,128)(2,1)S(1)}, bf16[64,256]{1,0:T(8,128)(2,1)S(1)}, u32[]{:S(2)}, u32[]{:S(2)}) collective-permute-start(bf16[64,256]{1,0:T(8,128)(2,1)S(1)} %collective-permute-done.17), channel_id=1, source_target_pairs={{0,64},{16,80},{32,96},{48,112},{64,0},{80,16},{96,32},{112,48},{1... | collective-permute-start | bytes 98312 | tf_op jit(solution)/shard_map/ppermute | solution.py:20
  129.3 5.8 collective-permute-start.19
  135.1 7.3 %collective-permute-start.20 = (bf16[64,256]{1,0:T(8,128)(2,1)S(1)}, bf16[64,256]{1,0:T(8,128)(2,1)S(1)}, u32[]{:S(2)}, u32[]{:S(2)}) collective-permute-start(bf16[64,256]{1,0:T(8,128)(2,1)S(1)} %collective-permute-done.19), channel_id=1, source_target_pairs={{0,256},{16,272},{32,288},{48,304},{64,320},{80,336},{96,352},{112... | collective-permute-start | bytes 98312 | tf_op jit(solution)/shard_map/ppermute | solution.py:20
  143.0 442.3 %reduce-scatter.4.cloned.1.call-start = ((), (), s32[]{:S(2)}) async-start(), calls=%async_computation.5 | async-start | bytes 2162688
  143.4 3.8 collective-permute-start.5
  147.2 15.8 %collective-permute-start.6 = (bf16[64,2048]{0,1:T(8,128)(2,1)S(1)}, bf16[64,2048]{0,1:T(8,128)(2,1)S(1)}, u32[]{:S(2)}, u32[]{:S(2)}) collective-permute-start(bf16[64,2048]{0,1:T(8,128)(2,1)S(1)} %collective-permute-done.5), channel_id=1, source_target_pairs={{0,32},{16,48},{32,0},{48,16},{64,96},{80,112},{96,64},{112,80},{1... | collective-permute-start | bytes 786440 | tf_op jit(solution)/shard_map/ppermute | solution.py:20
  163.1 17.2 %collective-permute-start.7 = (bf16[64,2048]{0,1:T(8,128)(2,1)S(1)}, bf16[64,2048]{0,1:T(8,128)(2,1)S(1)}, u32[]{:S(2)}, u32[]{:S(2)}) collective-permute-start(bf16[64,2048]{0,1:T(8,128)(2,1)S(1)} %collective-permute-done.6), channel_id=1, source_target_pairs={{0,64},{16,80},{32,96},{48,112},{64,0},{80,16},{96,32},{112,48},{1... | collective-permute-start | bytes 786440 | tf_op jit(solution)/shard_map/ppermute | solution.py:20
  180.3 14.1 %collective-permute-start.8 = (bf16[64,2048]{0,1:T(8,128)(2,1)S(1)}, bf16[64,2048]{0,1:T(8,128)(2,1)S(1)}, u32[]{:S(2)}, u32[]{:S(2)}) collective-permute-start(bf16[64,2048]{0,1:T(8,128)(2,1)S(1)} %collective-permute-done.7), channel_id=1, source_target_pairs={{0,128},{16,144},{32,160},{48,176},{64,192},{80,208},{96,224},{112... | collective-permute-start | bytes 786440 | tf_op jit(solution)/shard_map/ppermute | solution.py:20
  194.4 19.0 %collective-permute-start.9 = (bf16[64,2048]{0,1:T(8,128)(2,1)S(1)}, bf16[64,2048]{0,1:T(8,128)(2,1)S(1)}, u32[]{:S(2)}, u32[]{:S(2)}) collective-permute-start(bf16[64,2048]{0,1:T(8,128)(2,1)S(1)} %collective-permute-done.8), channel_id=1, source_target_pairs={{0,256},{16,272},{32,288},{48,304},{64,320},{80,336},{96,352},{112... | collective-permute-start | bytes 786440 | tf_op jit(solution)/shard_map/ppermute | solution.py:20
  200.3 3.1 collective-permute-start.11
  203.4 5.5 collective-permute-start.12
  208.8 7.0 %collective-permute-start.13 = (bf16[64,2]{0,1:T(2,128)(2,1)S(1)}, bf16[64,2]{0,1:T(2,128)(2,1)S(1)}, u32[]{:S(2)}, u32[]{:S(2)}) collective-permute-start(bf16[64,2]{0,1:T(2,128)(2,1)S(1)} %collective-permute-done.12), channel_id=1, source_target_pairs={{0,64},{16,80},{32,96},{48,112},{64,0},{80,16},{96,32},{112,48},{1... | collective-permute-start | bytes 776 | tf_op jit(solution)/shard_map/ppermute | solution.py:20
  215.8 5.6 collective-permute-start.14
  221.4 60.3 %collective-permute-start.15 = (bf16[64,2]{0,1:T(2,128)(2,1)S(1)}, bf16[64,2]{0,1:T(2,128)(2,1)S(1)}, u32[]{:S(2)}, u32[]{:S(2)}) collective-permute-start(bf16[64,2]{0,1:T(2,128)(2,1)S(1)} %collective-permute-done.14), channel_id=1, source_target_pairs={{0,256},{16,272},{32,288},{48,304},{64,320},{80,336},{96,352},{112... | collective-permute-start | bytes 776 | tf_op jit(solution)/shard_map/ppermute | solution.py:20
  437.6 3.4 collective-permute-start.21
  441.0 10.4 %collective-permute-start.22 = (bf16[64,2048]{1,0:T(8,128)(2,1)S(1)}, bf16[64,2048]{1,0:T(8,128)(2,1)S(1)}, u32[]{:S(2)}, u32[]{:S(2)}) collective-permute-start(bf16[64,2048]{1,0:T(8,128)(2,1)S(1)} %collective-permute-done.21), channel_id=1, source_target_pairs={{0,32},{16,48},{32,0},{48,16},{64,96},{80,112},{96,64},{112,80},{1... | collective-permute-start | bytes 786440 | tf_op jit(solution)/shard_map/ppermute | solution.py:20
  451.5 11.1 %collective-permute-start.23 = (bf16[64,2048]{1,0:T(8,128)(2,1)S(1)}, bf16[64,2048]{1,0:T(8,128)(2,1)S(1)}, u32[]{:S(2)}, u32[]{:S(2)}) collective-permute-start(bf16[64,2048]{1,0:T(8,128)(2,1)S(1)} %collective-permute-done.22), channel_id=1, source_target_pairs={{0,64},{16,80},{32,96},{48,112},{64,0},{80,16},{96,32},{112,48},{1... | collective-permute-start | bytes 786440 | tf_op jit(solution)/shard_map/ppermute | solution.py:20
  462.5 123.7 %collective-permute-start.24 = (bf16[64,2048]{1,0:T(8,128)(2,1)S(1)}, bf16[64,2048]{1,0:T(8,128)(2,1)S(1)}, u32[]{:S(2)}, u32[]{:S(2)}) collective-permute-start(bf16[64,2048]{1,0:T(8,128)(2,1)S(1)} %collective-permute-done.23), channel_id=1, source_target_pairs={{0,128},{16,144},{32,160},{48,176},{64,192},{80,208},{96,224},{112... | collective-permute-start | bytes 786440 | tf_op jit(solution)/shard_map/ppermute | solution.py:20
  586.2 33.1 %collective-permute-start.25 = (bf16[64,2048]{1,0:T(8,128)(2,1)S(1)}, bf16[64,2048]{1,0:T(8,128)(2,1)S(1)}, u32[]{:S(2)}, u32[]{:S(2)}) collective-permute-start(bf16[64,2048]{1,0:T(8,128)(2,1)S(1)} %collective-permute-done.24), channel_id=1, source_target_pairs={{0,256},{16,272},{32,288},{48,304},{64,320},{80,336},{96,352},{112... | collective-permute-start | bytes 786440 | tf_op jit(solution)/shard_map/ppermute | solution.py:20
  590.9 3.0 collective-permute-start.26
  593.9 5.5 collective-permute-start.27
  599.4 7.0 %collective-permute-start.28 = (bf16[64,2]{0,1:T(2,128)(2,1)S(1)}, bf16[64,2]{0,1:T(2,128)(2,1)S(1)}, u32[]{:S(2)}, u32[]{:S(2)}) collective-permute-start(bf16[64,2]{0,1:T(2,128)(2,1)S(1)} %collective-permute-done.27), channel_id=1, source_target_pairs={{0,64},{16,80},{32,96},{48,112},{64,0},{80,16},{96,32},{112,48},{1... | collective-permute-start | bytes 776 | tf_op jit(solution)/shard_map/ppermute | solution.py:20
  606.3 5.5 collective-permute-start.29
  611.8 7.0 %collective-permute-start.30 = (bf16[64,2]{0,1:T(2,128)(2,1)S(1)}, bf16[64,2]{0,1:T(2,128)(2,1)S(1)}, u32[]{:S(2)}, u32[]{:S(2)}) collective-permute-start(bf16[64,2]{0,1:T(2,128)(2,1)S(1)} %collective-permute-done.29), channel_id=1, source_target_pairs={{0,256},{16,272},{32,288},{48,304},{64,320},{80,336},{96,352},{112... | collective-permute-start | bytes 776 | tf_op jit(solution)/shard_map/ppermute | solution.py:20
Sparse Core Ops, SparseCore 0:
  11.1 65.4 all-gather.5
  81.4 60.2 all-reduce.1
  144.7 69.4 all-gather.3
  217.2 60.1 all-gather.7
  482.7 102.5 reduce-scatter.3
where the time goes:
time: 629 us; the launch traced here: 627 us
  waiting for transfers between devices  319 us (51%)
  starting transfers between devices  110 us (17%)
  local copies, waits for them, and re-layouts  77.6 us (12%)
  matrix products  40.3 us (6%)
  other arithmetic  27.1 us (4%)
  blocking collectives  20.7 us (3%)
  loops' own time  17.6 us (3%)
  between operations  14.3 us (2%)
    ppermute x30, starting transfers between devices, partner(): lax.ppermute(x, axis, [(i, i ^ 1 << distance) for i in range(lax.axis_siz...  108 us
    unnamed x6, waiting for transfers between devices  103 us
    ppermute x30, waiting for transfers between devices, partner(): lax.ppermute(x, axis, [(i, i ^ 1 << distance) for i in range(lax.axis_siz...  103 us
    all_gather x1, waiting for transfers between devices, per_device(): lax.all_gather(gate_in, 'seq', axis=1, tiled=True)  64 us
    gather x16, local copies, waits for them, and re-layouts, visibility(): key_segments = jnp.take(segment_ids, places)  50.3 us
    all_gather x1, waiting for transfers between devices, per_device(): lax.all_gather(own_values, 'seq', axis=0, tiled=True)  49.2 us
    dot_general x12, matrix products, block_scores(): jnp.einsum('tgeh,kgh->getk', query_heads, key_block, preferred_element_ty...  24 us
    all_gather x1, blocking collectives, per_device(): lax.all_gather(own_bias, 'seq', axis=0, tiled=True)  20.7 us
  transfers between devices with their start and end apart: 36, of which 28 were waited for; matrix products, arithmetic and copies ran while one was open for 3% of the time, Pallas kernels for 0%

commit v1 on v0

--- a/solution.py
+++ b/solution.py
@@ -8,6 +8,11 @@
 KV_HEADS = 8
 HEAD_DIM = 128
 NEG_FILL = -1e30
+
+
+def swapped_in(shard, name, dim):
+    outgoing = jnp.stack([shard] * lax.axis_size(name))
+    return jnp.concatenate(lax.all_to_all(outgoing, name, 0, 0), axis=dim)
 
 
 def from_behind(block, axis, distance):
@@ -54,9 +59,7 @@
         )
     mixed_rows = summed.astype(jnp.bfloat16)
     partial_hidden = jnp.dot(
-        mixed_rows,
-        lax.all_gather(gate_in, "seq", axis=1, tiled=True),
-        preferred_element_type=jnp.float32,
+        mixed_rows, swapped_in(gate_in, "seq", 1), preferred_element_type=jnp.float32
     )
     kv_local = key_vectors.shape[1] // HEAD_DIM
     group_size = QUERY_HEADS // KV_HEADS

time: 629 us -> 595 us (0.946)
  waiting for transfers between devices: 319 us -> 280 us
    all_gather x1 -> x0, waiting for transfers between devices: 64 us -> none  [per_device(): lax.all_gather(gate_in, 'seq', axis=1, tiled=True)]
    all_to_all x0 -> x1, waiting for transfers between devices: none -> 49.3 us  [swapped_in(): return jnp.concatenate(lax.all_to_all(outgoing, name, 0, 0), axis=dim)]
    all_gather x1, waiting for transfers between devices: 49.2 us -> 17.8 us  [per_device(): lax.all_gather(own_values, 'seq', axis=0, tiled=True)]
    all_to_all x0 -> x1, starting transfers between devices: none -> 7.58 us  [swapped_in(): return jnp.concatenate(lax.all_to_all(outgoing, name, 0, 0), axis=dim)]
    ppermute x30, waiting for transfers between devices: 103 us -> 110 us  [partner(): lax.ppermute(x, axis, [(i, i ^ 1 << distance) for i in range(lax.axis_siz...]
    unnamed x6 -> x5, waiting for transfers between devices: 103 us -> 103 us
where the time goes in v1:
time: 595 us; the launch traced here: 593 us
  waiting for transfers between devices  280 us (47%)
  starting transfers between devices  114 us (19%)
  local copies, waits for them, and re-layouts  80.1 us (13%)
  matrix products  40.2 us (7%)
  other arithmetic  24.7 us (4%)
  blocking collectives  20.8 us (3%)
  loops' own time  17 us (3%)
  between operations  16.3 us (3%)
    ppermute x30, waiting for transfers between devices, partner(): lax.ppermute(x, axis, [(i, i ^ 1 << distance) for i in range(lax.axis_siz...  110 us
    ppermute x30, starting transfers between devices, partner(): lax.ppermute(x, axis, [(i, i ^ 1 << distance) for i in range(lax.axis_siz...  104 us
    unnamed x5, waiting for transfers between devices  103 us
    gather x16, local copies, waits for them, and re-layouts, visibility(): key_segments = jnp.take(segment_ids, places)  50.3 us
    all_to_all x1, waiting for transfers between devices, swapped_in(): return jnp.concatenate(lax.all_to_all(outgoing, name, 0, 0), axis=dim)  49.3 us
    dot_general x12, matrix products, block_scores(): jnp.einsum('tgeh,kgh->getk', query_heads, key_block, preferred_element_ty...  23.9 us
    all_gather x1, blocking collectives, per_device(): lax.all_gather(own_bias, 'seq', axis=0, tiled=True)  20.8 us
    all_gather x1, waiting for transfers between devices, per_device(): lax.all_gather(own_values, 'seq', axis=0, tiled=True)  17.8 us
  transfers between devices with their start and end apart: 36, of which 28 were waited for; matrix products, arithmetic and copies ran while one was open for 3% of the time, Pallas kernels for 0%

profile of v1, /device:TPU:32, one launch (start us, length us, event | category | flops | bytes accessed | tf_op | source)
XLA Modules:
  0.0 593.1 jit_solution(15315571958458670738)
XLA Ops:
  8.0 3.4 stack.2
  11.5 7.6 %all-to-all-start = ((bf16[32,2048,32]{1,2,0:T(8,128)(2,1)}), bf16[32,2048,32]{1,2,0:T(8,128)(2,1)}, u32[]{:S(2)}, u32[]{:S(2)}) async-start(bf16[32,2048,32]{1,2,0:T(8,128)(2,1)} %stack.2), calls=%async_computation | async-start | bytes 8388608 | tf_op jit(solution)/shard_map/all_to_all | solution.py:15
  22.2 49.3 %all-to-all-done = bf16[32,2048,32]{1,2,0:T(8,128)(2,1)} async-done(((bf16[32,2048,32]{1,2,0:T(8,128)(2,1)}), bf16[32,2048,32]{1,2,0:T(8,128)(2,1)}, u32[]{:S(2)}, u32[]{:S(2)}) %all-to-all-start) | async-done | bytes 4194336 | tf_op jit(solution)/shard_map/all_to_all | solution.py:15
  71.5 4.7 fusion.39
  79.6 4.3 collective-permute-start.1
  89.2 4.8 collective-permute-done.2
  95.9 4.2 collective-permute-done.3
  103.0 4.7 collective-permute-done.4
  111.6 3.7 collective-permute-start.17
  117.4 3.5 collective-permute-start.18
  120.9 3.8 collective-permute-done.18
  126.7 3.8 collective-permute-done.19
  133.4 4.5 collective-permute-done.20
  142.7 3.8 collective-permute-start.6
  146.5 12.9 %collective-permute-done.6 = bf16[64,2048]{0,1:T(8,128)(2,1)S(1)} collective-permute-done((bf16[64,2048]{0,1:T(8,128)(2,1)S(1)}, bf16[64,2048]{0,1:T(8,128)(2,1)S(1)}, u32[]{:S(2)}, u32[]{:S(2)}) %collective-permute-start.6) | collective-permute-done | bytes 262176 | tf_op jit(solution)/shard_map/ppermute | solution.py:25
  162.1 14.9 %collective-permute-done.7 = bf16[64,2048]{0,1:T(8,128)(2,1)S(1)} collective-permute-done((bf16[64,2048]{0,1:T(8,128)(2,1)S(1)}, bf16[64,2048]{0,1:T(8,128)(2,1)S(1)}, u32[]{:S(2)}, u32[]{:S(2)}) %collective-permute-start.7) | collective-permute-done | bytes 262176 | tf_op jit(solution)/shard_map/ppermute | solution.py:25
  177.0 3.1 collective-permute-start.8
  180.1 11.6 %collective-permute-done.8 = bf16[64,2048]{0,1:T(8,128)(2,1)S(1)} collective-permute-done((bf16[64,2048]{0,1:T(8,128)(2,1)S(1)}, bf16[64,2048]{0,1:T(8,128)(2,1)S(1)}, u32[]{:S(2)}, u32[]{:S(2)}) %collective-permute-start.8) | collective-permute-done | bytes 262176 | tf_op jit(solution)/shard_map/ppermute | solution.py:25
  191.7 4.6 collective-permute-start.9
  203.1 3.2 collective-permute-done.12
  206.3 4.8 collective-permute-start.13
  219.1 3.9 collective-permute-start.15
  226.0 17.8 %all-gather.5.cloned.1.call-done = bf16[4096,256]{1,0:T(8,128)(2,1)} async-done(((bf16[128,256]{1,0:T(8,128)(2,1)}), bf16[4096,256]{1,0:T(8,128)(2,1)}) %all-gather.5.cloned.1.call-update) | async-done | bytes 2097168 | tf_op jit(solution)/shard_map/all_gather | solution.py:112
  248.3 20.8 %all_gather.10 = bf16[4096,2]{0,1:T(2,128)(2,1)S(1)} all-gather(bf16[128,2]{0,1:T(2,128)(2,1)S(1)} %pad_maximum_fusion.4), channel_id=1, replica_groups=mesh['seq'=32,'heads'=4,'dp'=4] {'seq'}, dimensions={0}, use_global_device_ids=true | all-gather | bytes 16896 | tf_op jit(solution)/shard_map/all_gather | solution.py:113
  269.0 58.5 %while.38 = (s32[]{:T(128)}, f32[2,8,128]{2,1,0:T(8,128)S(1)}, f32[2,8,128]{2,1,0:T(8,128)S(1)}, s32[4096]{0:T(1024)S(1)}, s32[128]{0:T(128)S(1)}, /*index=5*/bf...) while((s32[]{:T(128)}, f32[2,8,128]{2,1,0:T(8,128)S(1)}, ...), condition=%wide.region_7.9_spmd.clone, body=%wide.region_1.8_spmd.clone.sunk | while | flops 279233152 | bytes 10043169 | solution.py:138
  269.0 3.1 gather_fusion
  273.7 3.4 conditional.6
  277.2 3.1 gather_fusion
  281.9 3.4 conditional.6
  285.4 3.1 gather_fusion
  290.1 3.4 conditional.6
  293.5 3.1 gather_fusion
  298.3 3.1 gather_fusion
  303.0 3.1 gather_fusion
  307.7 3.4 conditional.6
  311.2 3.1 gather_fusion
  315.9 3.4 conditional.6
  319.4 3.1 gather_fusion
  324.0 3.4 conditional.6
  327.6 75.0 %while.39 = (s32[]{:T(128)}, f32[128,2,8,128]{3,0,2,1:T(8,128)S(1)}, f32[8,512,2]{1,2,0:T(2,128)S(1)}, s32[8]{0:T(128)S(1)}, s32[4096]{0:T(1024)S(1)}, /*index=5...) while((s32[]{:T(128)}, ...), condition=%wide.region_13.15_spmd.clone, body=%wide.region_8.14_spmd.clone.sunk | while | flops 545829504 | bytes 7545635 | solution.py:169
  328.9 3.1 gather_fusion.1
  333.5 4.6 conditional.7
  339.4 3.1 gather_fusion.1
  344.0 4.6 conditional.7
  349.9 3.1 gather_fusion.1
  354.5 4.6 conditional.7
  360.4 3.1 gather_fusion.1
  366.4 3.1 gather_fusion.1
  372.3 3.1 gather_fusion.1
  376.9 4.6 conditional.7
  382.8 3.1 gather_fusion.1
  387.5 4.6 conditional.7
  393.4 3.1 gather_fusion.1
  398.0 4.6 conditional.7
  409.2 7.6 %collective-permute-done.22 = bf16[64,2048]{1,0:T(8,128)(2,1)S(1)} collective-permute-done((bf16[64,2048]{1,0:T(8,128)(2,1)S(1)}, bf16[64,2048]{1,0:T(8,128)(2,1)S(1)}, u32[]{:S(2)}, u32[]{:S(2)}) %collective-permute-start.22) | collective-permute-done | bytes 262176 | tf_op jit(solution)/shard_map/ppermute | solution.py:25
  416.9 4.3 collective-permute-start.23
  421.1 6.8 %collective-permute-done.23 = bf16[64,2048]{1,0:T(8,128)(2,1)S(1)} collective-permute-done((bf16[64,2048]{1,0:T(8,128)(2,1)S(1)}, bf16[64,2048]{1,0:T(8,128)(2,1)S(1)}, u32[]{:S(2)}, u32[]{:S(2)}) %collective-permute-start.23) | collective-permute-done | bytes 262176 | tf_op jit(solution)/shard_map/ppermute | solution.py:25
  427.9 17.9 %collective-permute-start.24 = (bf16[64,2048]{1,0:T(8,128)(2,1)S(1)}, bf16[64,2048]{1,0:T(8,128)(2,1)S(1)}, u32[]{:S(2)}, u32[]{:S(2)}) collective-permute-start(bf16[64,2048]{1,0:T(8,128)(2,1)S(1)} %collective-permute-done.23), channel_id=1, source_target_pairs={{0,128},{16,144},{32,160},{48,176},{64,192},{80,208},{96,224},{112... | collective-permute-start | bytes 786440 | tf_op jit(solution)/shard_map/ppermute | solution.py:25
  447.9 102.7 %reduce-scatter.4.cloned.1.call-done = f32[128,2]{1,0:T(8,128)} async-done(((f32[4096,2]{1,0:T(8,128)}), f32[128,2]{1,0:T(8,128)}) %reduce-scatter.4.cloned.1.call-update) | async-done | bytes 1040
  551.5 4.6 collective-permute-start.25
  561.2 3.5 collective-permute-done.27
  564.7 3.4 collective-permute-start.28
  568.1 3.6 collective-permute-done.28
  580.1 3.9 collective-permute-done.30
  (269 shorter events, 147.7 us)
Async XLA Ops:
  8.0 188.3 %copy-start = (bf16[1024,8]{0,1:T(8,128)(2,1)S(1)}, bf16[1024,8]{0,1:T(8,128)(2,1)}, u32[]{:S(2)}) copy-start(bf16[1024,8]{0,1:T(8,128)(2,1)} %param.21) | copy-start | bytes 49156
  11.5 7.6 %copy-start.2 = (bf16[128,2048]{1,0:T(8,128)(2,1)S(1)}, bf16[128,2048]{1,0:T(8,128)(2,1)}, u32[]{:S(2)}) copy-start(bf16[128,2048]{1,0:T(8,128)(2,1)} %param.18) | copy-start | bytes 1572868
  11.5 9.8 %copy-start.6 = (bf16[4,2048]{1,0:T(4,128)(2,1)S(1)}, bf16[4,2048]{1,0:T(4,128)(2,1)}, u32[]{:S(2)}) copy-start(bf16[4,2048]{1,0:T(4,128)(2,1)} %param.19) | copy-start | bytes 49156
  11.5 60.0 %all-to-all-start = ((bf16[32,2048,32]{1,2,0:T(8,128)(2,1)}), bf16[32,2048,32]{1,2,0:T(8,128)(2,1)}, u32[]{:S(2)}, u32[]{:S(2)}) async-start(bf16[32,2048,32]{1,2,0:T(8,128)(2,1)} %stack.2), calls=%async_computation | async-start | bytes 8388608 | tf_op jit(solution)/shard_map/all_to_all | solution.py:15
  19.0 177.3 %all-reduce.2.cloned.1.call-start = ((), (), s32[]{:S(2)}) async-start(), calls=%async_computation.3 | async-start | bytes 1048576 | tf_op jit(solution)/shard_map/psum | solution.py:67
  19.1 2.9 collective-permute-start.10
  71.5 4.8 copy-start.4
  71.5 37.0 %copy-start.5 = (bf16[128,256]{1,0:T(8,128)(2,1)S(1)}, bf16[128,256]{1,0:T(8,128)(2,1)}, u32[]{:S(2)}) copy-start(bf16[128,256]{1,0:T(8,128)(2,1)} %param.24) | copy-start | bytes 196612
  71.5 67.0 %copy-start.3 = (bf16[128,2048]{1,0:T(8,128)(2,1)S(1)}, bf16[128,2048]{1,0:T(8,128)(2,1)}, u32[]{:S(2)}) copy-start(bf16[128,2048]{1,0:T(8,128)(2,1)} %param.22) | copy-start | bytes 1572868
  76.2 123.5 %copy-start.1 = (s32[4096]{0:T(1024)S(1)}, s32[4096]{0:T(1024)}, u32[]{:S(2)}) copy-start(s32[4096]{0:T(1024)} %param.25) | copy-start | bytes 49156
  76.2 140.4 %all-gather.3.cloned.1.call-start = ((), (), s32[]{:S(2)}) async-start(), calls=%async_computation.2 | async-start | bytes 2162688 | tf_op jit(solution)/shard_map/all_gather | solution.py:111
  76.4 3.1 collective-permute-start
  79.6 6.7 %collective-permute-start.1 = (bf16[64,256]{0,1:T(8,128)(2,1)S(1)}, bf16[64,256]{0,1:T(8,128)(2,1)S(1)}, u32[]{:S(2)}, u32[]{:S(2)}) collective-permute-start(bf16[64,256]{0,1:T(8,128)(2,1)S(1)} %collective-permute-done), channel_id=1, source_target_pairs={{0,32},{16,48},{32,0},{48,16},{64,96},{80,112},{96,64},{112,80},{1... | collective-permute-start | bytes 98312 | tf_op jit(solution)/shard_map/ppermute | solution.py:25
  86.3 7.7 %collective-permute-start.2 = (bf16[64,256]{0,1:T(8,128)(2,1)S(1)}, bf16[64,256]{0,1:T(8,128)(2,1)S(1)}, u32[]{:S(2)}, u32[]{:S(2)}) collective-permute-start(bf16[64,256]{0,1:T(8,128)(2,1)S(1)} %collective-permute-done.1), channel_id=1, source_target_pairs={{0,64},{16,80},{32,96},{48,112},{64,0},{80,16},{96,32},{112,48},{1... | collective-permute-start | bytes 98312 | tf_op jit(solution)/shard_map/ppermute | solution.py:25
  93.9 6.1 %collective-permute-start.3 = (bf16[64,256]{0,1:T(8,128)(2,1)S(1)}, bf16[64,256]{0,1:T(8,128)(2,1)S(1)}, u32[]{:S(2)}, u32[]{:S(2)}) collective-permute-start(bf16[64,256]{0,1:T(8,128)(2,1)S(1)} %collective-permute-done.2), channel_id=1, source_target_pairs={{0,128},{16,144},{32,160},{48,176},{64,192},{80,208},{96,224},{112... | collective-permute-start | bytes 98312 | tf_op jit(solution)/shard_map/ppermute | solution.py:25
  100.1 7.7 %collective-permute-start.4 = (bf16[64,256]{0,1:T(8,128)(2,1)S(1)}, bf16[64,256]{0,1:T(8,128)(2,1)S(1)}, u32[]{:S(2)}, u32[]{:S(2)}) collective-permute-start(bf16[64,256]{0,1:T(8,128)(2,1)S(1)} %collective-permute-done.3), channel_id=1, source_target_pairs={{0,256},{16,272},{32,288},{48,304},{64,320},{80,336},{96,352},{112... | collective-permute-start | bytes 98312 | tf_op jit(solution)/shard_map/ppermute | solution.py:25
  108.5 135.4 %all-gather.5.cloned.1.call-start = ((), (), s32[]{:S(2)}) async-start(), calls=%async_computation.4 | async-start | bytes 2162688 | tf_op jit(solution)/shard_map/all_gather | solution.py:112
  108.5 3.1 collective-permute-start.16
  111.6 5.8 collective-permute-start.17
  117.4 7.3 %collective-permute-start.18 = (bf16[64,256]{1,0:T(8,128)(2,1)S(1)}, bf16[64,256]{1,0:T(8,128)(2,1)S(1)}, u32[]{:S(2)}, u32[]{:S(2)}) collective-permute-start(bf16[64,256]{1,0:T(8,128)(2,1)S(1)} %collective-permute-done.17), channel_id=1, source_target_pairs={{0,64},{16,80},{32,96},{48,112},{64,0},{80,16},{96,32},{112,48},{1... | collective-permute-start | bytes 98312 | tf_op jit(solution)/shard_map/ppermute | solution.py:25
  124.7 5.8 collective-permute-start.19
  130.5 7.3 %collective-permute-start.20 = (bf16[64,256]{1,0:T(8,128)(2,1)S(1)}, bf16[64,256]{1,0:T(8,128)(2,1)S(1)}, u32[]{:S(2)}, u32[]{:S(2)}) collective-permute-start(bf16[64,256]{1,0:T(8,128)(2,1)S(1)} %collective-permute-done.19), channel_id=1, source_target_pairs={{0,256},{16,272},{32,288},{48,304},{64,320},{80,336},{96,352},{112... | collective-permute-start | bytes 98312 | tf_op jit(solution)/shard_map/ppermute | solution.py:25
  138.5 412.1 %reduce-scatter.4.cloned.1.call-start = ((), (), s32[]{:S(2)}) async-start(), calls=%async_computation.5 | async-start | bytes 2162688
  138.9 3.8 collective-permute-start.5
  142.7 16.7 %collective-permute-start.6 = (bf16[64,2048]{0,1:T(8,128)(2,1)S(1)}, bf16[64,2048]{0,1:T(8,128)(2,1)S(1)}, u32[]{:S(2)}, u32[]{:S(2)}) collective-permute-start(bf16[64,2048]{0,1:T(8,128)(2,1)S(1)} %collective-permute-done.5), channel_id=1, source_target_pairs={{0,32},{16,48},{32,0},{48,16},{64,96},{80,112},{96,64},{112,80},{1... | collective-permute-start | bytes 786440 | tf_op jit(solution)/shard_map/ppermute | solution.py:25
  159.4 17.6 %collective-permute-start.7 = (bf16[64,2048]{0,1:T(8,128)(2,1)S(1)}, bf16[64,2048]{0,1:T(8,128)(2,1)S(1)}, u32[]{:S(2)}, u32[]{:S(2)}) collective-permute-start(bf16[64,2048]{0,1:T(8,128)(2,1)S(1)} %collective-permute-done.6), channel_id=1, source_target_pairs={{0,64},{16,80},{32,96},{48,112},{64,0},{80,16},{96,32},{112,48},{1... | collective-permute-start | bytes 786440 | tf_op jit(solution)/shard_map/ppermute | solution.py:25
  177.0 14.7 %collective-permute-start.8 = (bf16[64,2048]{0,1:T(8,128)(2,1)S(1)}, bf16[64,2048]{0,1:T(8,128)(2,1)S(1)}, u32[]{:S(2)}, u32[]{:S(2)}) collective-permute-start(bf16[64,2048]{0,1:T(8,128)(2,1)S(1)} %collective-permute-done.7), channel_id=1, source_target_pairs={{0,128},{16,144},{32,160},{48,176},{64,192},{80,208},{96,224},{112... | collective-permute-start | bytes 786440 | tf_op jit(solution)/shard_map/ppermute | solution.py:25
  191.7 19.4 %collective-permute-start.9 = (bf16[64,2048]{0,1:T(8,128)(2,1)S(1)}, bf16[64,2048]{0,1:T(8,128)(2,1)S(1)}, u32[]{:S(2)}, u32[]{:S(2)}) collective-permute-start(bf16[64,2048]{0,1:T(8,128)(2,1)S(1)} %collective-permute-done.8), channel_id=1, source_target_pairs={{0,256},{16,272},{32,288},{48,304},{64,320},{80,336},{96,352},{112... | collective-permute-start | bytes 786440 | tf_op jit(solution)/shard_map/ppermute | solution.py:25
  197.7 3.1 collective-permute-start.11
  200.9 5.5 collective-permute-start.12
  206.3 7.0 %collective-permute-start.13 = (bf16[64,2]{0,1:T(2,128)(2,1)S(1)}, bf16[64,2]{0,1:T(2,128)(2,1)S(1)}, u32[]{:S(2)}, u32[]{:S(2)}) collective-permute-start(bf16[64,2]{0,1:T(2,128)(2,1)S(1)} %collective-permute-done.12), channel_id=1, source_target_pairs={{0,64},{16,80},{32,96},{48,112},{64,0},{80,16},{96,32},{112,48},{1... | collective-permute-start | bytes 776 | tf_op jit(solution)/shard_map/ppermute | solution.py:25
  213.3 5.8 collective-permute-start.14
  219.1 29.0 %collective-permute-start.15 = (bf16[64,2]{0,1:T(2,128)(2,1)S(1)}, bf16[64,2]{0,1:T(2,128)(2,1)S(1)}, u32[]{:S(2)}, u32[]{:S(2)}) collective-permute-start(bf16[64,2]{0,1:T(2,128)(2,1)S(1)} %collective-permute-done.14), channel_id=1, source_target_pairs={{0,256},{16,272},{32,288},{48,304},{64,320},{80,336},{96,352},{112... | collective-permute-start | bytes 776 | tf_op jit(solution)/shard_map/ppermute | solution.py:25
  403.0 3.4 collective-permute-start.21
  406.4 10.4 %collective-permute-start.22 = (bf16[64,2048]{1,0:T(8,128)(2,1)S(1)}, bf16[64,2048]{1,0:T(8,128)(2,1)S(1)}, u32[]{:S(2)}, u32[]{:S(2)}) collective-permute-start(bf16[64,2048]{1,0:T(8,128)(2,1)S(1)} %collective-permute-done.21), channel_id=1, source_target_pairs={{0,32},{16,48},{32,0},{48,16},{64,96},{80,112},{96,64},{112,80},{1... | collective-permute-start | bytes 786440 | tf_op jit(solution)/shard_map/ppermute | solution.py:25
  416.9 11.1 %collective-permute-start.23 = (bf16[64,2048]{1,0:T(8,128)(2,1)S(1)}, bf16[64,2048]{1,0:T(8,128)(2,1)S(1)}, u32[]{:S(2)}, u32[]{:S(2)}) collective-permute-start(bf16[64,2048]{1,0:T(8,128)(2,1)S(1)} %collective-permute-done.22), channel_id=1, source_target_pairs={{0,64},{16,80},{32,96},{48,112},{64,0},{80,16},{96,32},{112,48},{1... | collective-permute-start | bytes 786440 | tf_op jit(solution)/shard_map/ppermute | solution.py:25
  427.9 123.6 %collective-permute-start.24 = (bf16[64,2048]{1,0:T(8,128)(2,1)S(1)}, bf16[64,2048]{1,0:T(8,128)(2,1)S(1)}, u32[]{:S(2)}, u32[]{:S(2)}) collective-permute-start(bf16[64,2048]{1,0:T(8,128)(2,1)S(1)} %collective-permute-done.23), channel_id=1, source_target_pairs={{0,128},{16,144},{32,160},{48,176},{64,192},{80,208},{96,224},{112... | collective-permute-start | bytes 786440 | tf_op jit(solution)/shard_map/ppermute | solution.py:25
  551.5 33.1 %collective-permute-start.25 = (bf16[64,2048]{1,0:T(8,128)(2,1)S(1)}, bf16[64,2048]{1,0:T(8,128)(2,1)S(1)}, u32[]{:S(2)}, u32[]{:S(2)}) collective-permute-start(bf16[64,2048]{1,0:T(8,128)(2,1)S(1)} %collective-permute-done.24), channel_id=1, source_target_pairs={{0,256},{16,272},{32,288},{48,304},{64,320},{80,336},{96,352},{112... | collective-permute-start | bytes 786440 | tf_op jit(solution)/shard_map/ppermute | solution.py:25
  556.2 3.0 collective-permute-start.26
  559.2 5.5 collective-permute-start.27
  564.7 7.0 %collective-permute-start.28 = (bf16[64,2]{0,1:T(2,128)(2,1)S(1)}, bf16[64,2]{0,1:T(2,128)(2,1)S(1)}, u32[]{:S(2)}, u32[]{:S(2)}) collective-permute-start(bf16[64,2]{0,1:T(2,128)(2,1)S(1)} %collective-permute-done.27), channel_id=1, source_target_pairs={{0,64},{16,80},{32,96},{48,112},{64,0},{80,16},{96,32},{112,48},{1... | collective-permute-start | bytes 776 | tf_op jit(solution)/shard_map/ppermute | solution.py:25
  571.6 5.5 collective-permute-start.29
  577.1 7.0 %collective-permute-start.30 = (bf16[64,2]{0,1:T(2,128)(2,1)S(1)}, bf16[64,2]{0,1:T(2,128)(2,1)S(1)}, u32[]{:S(2)}, u32[]{:S(2)}) collective-permute-start(bf16[64,2]{0,1:T(2,128)(2,1)S(1)} %collective-permute-done.29), channel_id=1, source_target_pairs={{0,256},{16,272},{32,288},{48,304},{64,320},{80,336},{96,352},{112... | collective-permute-start | bytes 776 | tf_op jit(solution)/shard_map/ppermute | solution.py:25
Sparse Core Ops, SparseCore 0:
  76.3 64.1 all-reduce.1
Sparse Core Ops, SparseCore 1:
  108.5 70.2 all-gather.2
  181.8 61.9 all-gather.4
  448.0 102.6 reduce-scatter.3
